TPU v7x, 512 devices: a whole 4x8x8 slice. The times are simulated.
512 devices in a mesh: ka: 64 (over z_lo, y, core), rows: 8 (over x, z_hi).
Axes of the slice: x: 4, y: 8, z: 8 (z_hi: 2, z_lo: 4; z = z_hi * 4 + z_lo), core: 2. Of those that a mesh axis runs over, the one named last changes fastest.
Arguments:
- amplitudes: float32 [256, 64, 2, 2, 256], P('rows', 'ka'), may hold values from -6 to 6
- conduction_values: float32 [2, 512, 64, 256], P(None, 'rows', 'ka'), may hold values from -0.375 to 0.375
- valence_values: float32 [2, 512, 64, 256], P(None, 'rows', 'ka'), may hold values from -0.375 to 0.375
- screened: float32 [2, 64, 512, 512], P(None, None, 'ka', 'rows'), may hold values from -0.024 to 0.024
- conduction_energy: float32 [256, 64], P('rows', 'ka'), may hold values from 0.5 to 1
- valence_energy: float32 [64, 256], P('ka'), may hold values from -0.5 to 0
- offset_table: int32 [64, 64], replicated, may hold values from 0 to 63, as said below
Outputs:
- applied_once: float32 [256, 64, 2, 2, 256], P('rows', 'ka')
- applied_twice: float32 [256, 64, 2, 2, 256], P('rows', 'ka')
Inputs may be any that keep to these rules, and one draw needn't show every extreme that they name: offset_table[k, k2] = 4 * 4 * a + 4 * b + d, where (a, b, d) are the coordinates of the grid point of k-point k minus those of k-point k2, each modulo 4, for a one to one assignment of the 64 k-points to the points of a 4 x 4 x 4 grid.
All inputs are finite; a program needn't handle non-finite values.
Results may differ from a plain program's by a relative error of at most 0.0003.
Values sent between devices are 32-bit elements; how exact they have to be, the bound alone decides.
No kernel may reach another device: no remote copies, remote signals or barrier semaphores. Data moves between devices by JAX's collectives and lax.ppermute only.
A program may use at most 64 MiB of HBM per device.

v0:
```python
import math

import jax
import jax.numpy as jnp
from jax import lax
from jax.sharding import PartitionSpec as P

KG = 4


def product(formula, left, right):
    return jnp.einsum(formula, left, right, precision=lax.Precision.HIGHEST)


def complex_multiply(formula, left_pair, right_pair):
    real_part = product(formula, left_pair[0], right_pair[0]) - product(
        formula, left_pair[1], right_pair[1]
    )
    imag_part = product(formula, left_pair[0], right_pair[1]) + product(
        formula, left_pair[1], right_pair[0]
    )
    return (real_part, imag_part)


def conjugated_rows(pair):
    return (pair[0], -pair[1])


def decode(flat, grid_side):
    return jnp.stack(
        [flat // (grid_side * grid_side), flat // grid_side % grid_side, flat % grid_side], axis=0
    )


def phase_table(left_flat, right_flat, grid_side):
    turns = (
        jnp.sum(
            decode(left_flat, grid_side)[:, :, None] * decode(right_flat, grid_side)[:, None, :],
            axis=0,
        )
        % grid_side
    )
    angle = turns.astype(jnp.float32) * (2.0 * math.pi / grid_side)
    return (jnp.cos(angle), -jnp.sin(angle))


def spectral(kernel_block, weight_pair, forward):
    moments = complex_multiply("rk,sknm->srnm", forward, (kernel_block[0], kernel_block[1]))
    scaled_real = weight_pair[0][None] * moments[0] - weight_pair[1][None] * moments[1]
    scaled_imag = weight_pair[0][None] * moments[1] + weight_pair[1][None] * moments[0]
    result = complex_multiply("rk,srnm->sknm", conjugated_rows(forward), (scaled_real, scaled_imag))
    return jnp.stack(result, axis=0) / forward[0].shape[0]


def expand(mixed_component, valence_component):
    orbital_pairs = complex_multiply(
        "zudg,cug->zucd", mixed_component, conjugated_rows(valence_component)
    )
    return jnp.stack(orbital_pairs, axis=0)


def contract(kernel_block, valence_component):
    return complex_multiply("bxra,rxo->bxao", (kernel_block[0], kernel_block[1]), valence_component)


def per_device(
    amplitudes,
    conduction_values,
    valence_values,
    screened,
    conduction_energy,
    valence_energy,
    offset_table,
):
    points_all = lax.all_gather(valence_values, "rows", axis=1, tiled=True)
    valence_couple = (points_all[0], points_all[1])
    cond_pair = (conduction_values[0], conduction_values[1])
    frequencies = jnp.arange(offset_table.shape[0], dtype=jnp.int32)
    forward = phase_table(frequencies, offset_table[:, 0], KG)
    forward_grid = phase_table(frequencies, frequencies, KG)
    weights = complex_multiply("rq,qnm->rnm", forward_grid, (screened[0], screened[1]))
    energy = (conduction_energy[:, :, None] - valence_energy[None])[:, :, None, None, :]

    def apply(state):
        whole = lax.all_gather(state, "rows", axis=0, tiled=True)
        mixed_orbitals = complex_multiply(
            "mkc,cksv->skmv", cond_pair, (whole[:, :, 0], whole[:, :, 1])
        )
        results = []
        for member in range(state.shape[3]):
            chosen = tuple((part[member : member + 1] for part in mixed_orbitals))
            sent = lax.all_to_all(
                expand(chosen, valence_couple), "ka", split_axis=3, concat_axis=2, tiled=True
            )
            back = lax.all_to_all(
                spectral(sent, weights, forward), "ka", split_axis=2, concat_axis=3, tiled=True
            )
            results.append(contract(back, valence_couple))
        summed_terms = tuple(
            (
                jnp.concatenate([entry[component] for entry in results], axis=0)
                for component in range(2)
            )
        )
        sliced = tuple((part for part in cond_pair))
        result = complex_multiply("mkc,skmv->cksv", conjugated_rows(sliced), summed_terms)
        kernel = lax.psum_scatter(
            jnp.stack(result, axis=2), "rows", scatter_dimension=0, tiled=True
        )
        return energy * state + kernel

    first = apply(amplitudes)
    return (first, apply(first))


def solution(mesh):
    placed = (
        P("rows", "ka", None, None, None),
        P(None, "rows", "ka", None),
        P(None, "rows", "ka", None),
        P(None, None, "ka", "rows"),
        P("rows", "ka"),
        P("ka", None),
        P(),
    )
    return jax.shard_map(
        per_device,
        mesh=mesh,
        in_specs=placed,
        out_specs=(P("rows", "ka", None, None, None), P("rows", "ka", None, None, None)),
        check_vma=False,
    )
```

profile of v0, /device:TPU:72, one launch (start us, length us, event | category | flops | bytes accessed | tf_op | source)
XLA Modules:
  0.0 714.2 jit_solution(13609223937029588765)
XLA Ops:
  12.6 68.8 %all-gather.6.cloned.1.call-done = f32[2,512,1,256]{3,2,1,0:T(1,128)} async-done(((f32[2,64,1,256]{3,2,1,0:T(1,128)}), f32[2,512,1,256]{3,2,1,0:T(1,128)}) %all-gather.6.cloned.1.call-update) | async-done | bytes 1048592 | tf_op jit(solution)/shard_map/all_gather | solution.py:75
  81.4 2.3 fusion.284
  83.7 64.7 %all-gather.4.cloned.1.call-done = f32[256,1,2,2,256]{4,0,3,2,1:T(8,128)} async-done(((f32[32,1,2,2,256]{4,0,3,2,1:T(8,128)}), f32[256,1,2,2,256]{4,0,3,2,1:T(8,128)}) %all-gather.4.cloned.1.call-update) | async-done | bytes 1048592 | tf_op jit(solution)/shard_map/all_gather | solution.py:85
  157.1 2.4 reduce.2
  160.8 10.1 %all-to-all-start = ((f32[64,1,1024]{2,1,0:T(1,128)}), f32[64,1,1024]{2,1,0:T(1,128)}, u32[]{:S(2)}, u32[]{:S(2)}) async-start(f32[64,1,1024]{2,1,0:T(1,128)} %reshape.1066), calls=%async_computation | async-start | bytes 524288 | tf_op jit(solution)/shard_map/all_to_all | solution.py:92
  173.1 2.4 reduce.4
  176.8 5.2 all-to-all-done
  182.0 6.6 all-to-all-start.2
  188.6 2.2 reduce.3
  196.0 3.9 all-to-all-done.2
  199.8 2.9 reduce.5
  202.7 1.6 reshape.1063
  216.5 2.1 reshape.1068
  218.6 7.3 %all-to-all-start.1 = ((f32[64,1,1024]{2,1,0:T(1,128)}), f32[64,1,1024]{2,1,0:T(1,128)S(1)}, u32[]{:S(2)}, u32[]{:S(2)}) async-start(f32[64,1,1024]{2,1,0:T(1,128)} %reshape.1068), calls=%async_computation.1 | async-start | bytes 524288 | tf_op jit(solution)/shard_map/all_to_all | solution.py:95
  229.8 7.4 %all-to-all-done.1 = f32[64,1,1024]{2,1,0:T(1,128)S(1)} async-done(((f32[64,1,1024]{2,1,0:T(1,128)}), f32[64,1,1024]{2,1,0:T(1,128)S(1)}, u32[]{:S(2)}, u32[]{:S(2)}) %all-to-all-start.1) | async-done | bytes 262176 | tf_op jit(solution)/shard_map/all_to_all | solution.py:95
  237.2 6.4 all-to-all-start.3
  246.2 8.7 %all-to-all-done.3 = f32[64,1,1024]{2,1,0:T(1,128)S(1)} async-done(((f32[64,1,1024]{2,1,0:T(1,128)}), f32[64,1,1024]{2,1,0:T(1,128)S(1)}, u32[]{:S(2)}, u32[]{:S(2)}) %all-to-all-start.3) | async-done | bytes 262176 | tf_op jit(solution)/shard_map/all_to_all | solution.py:95
  266.7 132.5 %all-reduce.5.cloned.1.call-done = f32[256,1,2,2,256]{4,3,2,1,0:T(2,128)} async-done(((f32[256,1,2,2,256]{4,3,2,1,0:T(2,128)}), f32[256,1,2,2,256]{4,3,2,1,0:T(2,128)}) %all-reduce.5.cloned.1.call-update) | async-done | bytes 1048592
  399.2 1.6 dynamic-slice_add_fusion.1
  400.8 63.3 %all-gather.8.cloned.1.call-done = f32[256,1,2,2,256]{4,3,2,1,0:T(2,128)} async-done(((f32[32,1,2,2,256]{4,3,2,1,0:T(2,128)}), f32[256,1,2,2,256]{4,3,2,1,0:T(2,128)}) %all-gather.8.cloned.1.call-update) | async-done | bytes 1048592 | tf_op jit(solution)/shard_map/all_gather | solution.py:85
  471.0 2.4 reduce.8
  474.7 9.4 %all-to-all-start.4 = ((f32[64,1,1024]{2,1,0:T(1,128)}), f32[64,1,1024]{2,1,0:T(1,128)S(1)}, u32[]{:S(2)}, u32[]{:S(2)}) async-start(f32[64,1,1024]{2,1,0:T(1,128)} %reshape.1074), calls=%async_computation.4 | async-start | bytes 524288 | tf_op jit(solution)/shard_map/all_to_all | solution.py:92
  486.4 2.4 reduce.10
  490.1 5.4 all-to-all-done.4
  495.5 6.4 all-to-all-start.6
  507.3 5.9 all-to-all-done.6
  526.1 6.3 all-to-all-start.5
  536.3 7.4 %all-to-all-done.5 = f32[64,1,1024]{2,1,0:T(1,128)S(1)} async-done(((f32[64,1,1024]{2,1,0:T(1,128)}), f32[64,1,1024]{2,1,0:T(1,128)S(1)}, u32[]{:S(2)}, u32[]{:S(2)}) %all-to-all-start.5) | async-done | bytes 262176 | tf_op jit(solution)/shard_map/all_to_all | solution.py:95
  543.8 6.4 all-to-all-start.7
  552.7 8.7 %all-to-all-done.7 = f32[64,1,1024]{2,1,0:T(1,128)S(1)} async-done(((f32[64,1,1024]{2,1,0:T(1,128)}), f32[64,1,1024]{2,1,0:T(1,128)S(1)}, u32[]{:S(2)}, u32[]{:S(2)}) %all-to-all-start.7) | async-done | bytes 262176 | tf_op jit(solution)/shard_map/all_to_all | solution.py:95
  570.3 135.5 %all-reduce.7.cloned.1.call-done = f32[256,1,2,2,256]{4,3,2,1,0:T(2,128)} async-done(((f32[256,1,2,2,256]{4,3,2,1,0:T(2,128)}), f32[256,1,2,2,256]{4,3,2,1,0:T(2,128)}) %all-reduce.7.cloned.1.call-update) | async-done | bytes 1048592
  705.8 1.6 dynamic-slice_add_fusion
  (188 shorter events, 98.3 us)
Async XLA Ops:
  7.2 0.9 copy-start.8
  7.2 2.7 copy-start.7
  7.2 74.2 %all-gather.6.cloned.1.call-start = ((), (), s32[]{:S(2)}) async-start(), calls=%async_computation.9 | async-start | bytes 1179648 | tf_op jit(solution)/shard_map/all_gather | solution.py:75
  7.9 140.5 %all-gather.4.cloned.1.call-start = ((), (), s32[]{:S(2)}) async-start(), calls=%async_computation.8 | async-start | bytes 1179648 | tf_op jit(solution)/shard_map/all_gather | solution.py:85
  10.4 0.9 copy-start.11
  151.4 2.5 copy-start
  154.9 0.7 copy-start.2
  160.8 10.1 %copy-start.3 = (f32[2,1,64,256]{3,2,0,1:T(8,128)S(1)}, f32[2,1,64,256]{3,2,0,1:T(8,128)}, u32[]{:S(2)}) copy-start(f32[2,1,64,256]{3,2,0,1:T(8,128)} %copy-done.2) | copy-start | bytes 393220
  160.8 10.1 %copy-start.10 = (f32[64,512]{1,0:T(8,128)S(1)}, f32[64,512]{1,0:T(8,128)}, u32[]{:S(2)}) copy-start(f32[64,512]{1,0:T(8,128)} %fusion.60) | copy-start | bytes 393220
  160.8 21.2 %all-to-all-start = ((f32[64,1,1024]{2,1,0:T(1,128)}), f32[64,1,1024]{2,1,0:T(1,128)}, u32[]{:S(2)}, u32[]{:S(2)}) async-start(f32[64,1,1024]{2,1,0:T(1,128)} %reshape.1066), calls=%async_computation | async-start | bytes 524288 | tf_op jit(solution)/shard_map/all_to_all | solution.py:92
  182.0 17.8 %all-to-all-start.2 = ((f32[64,1,1024]{2,1,0:T(1,128)}), f32[64,1,1024]{2,1,0:T(1,128)}, u32[]{:S(2)}, u32[]{:S(2)}) async-start(f32[64,1,1024]{2,1,0:T(1,128)} %reshape.1062), calls=%async_computation.2 | async-start | bytes 524288 | tf_op jit(solution)/shard_map/all_to_all | solution.py:92
  210.5 1.0 copy-start.5
  218.6 18.6 %all-to-all-start.1 = ((f32[64,1,1024]{2,1,0:T(1,128)}), f32[64,1,1024]{2,1,0:T(1,128)S(1)}, u32[]{:S(2)}, u32[]{:S(2)}) async-start(f32[64,1,1024]{2,1,0:T(1,128)} %reshape.1068), calls=%async_computation.1 | async-start | bytes 524288 | tf_op jit(solution)/shard_map/all_to_all | solution.py:95
  237.2 17.7 %all-to-all-start.3 = ((f32[64,1,1024]{2,1,0:T(1,128)}), f32[64,1,1024]{2,1,0:T(1,128)S(1)}, u32[]{:S(2)}, u32[]{:S(2)}) async-start(f32[64,1,1024]{2,1,0:T(1,128)} %reshape.1064), calls=%async_computation.3 | async-start | bytes 524288 | tf_op jit(solution)/shard_map/all_to_all | solution.py:95
  243.6 155.6 %all-reduce.5.cloned.1.call-start = ((), (), s32[]{:S(2)}) async-start(), calls=%async_computation.11 | async-start | bytes 2097152
  263.8 135.4 %copy-start.9 = (f32[32,1,2,2,256]{4,3,2,1,0:T(2,128)S(1)}, f32[32,1,2,2,256]{4,3,2,1,0:T(2,128)}, u32[]{:S(2)}) copy-start(f32[32,1,2,2,256]{4,3,2,1,0:T(2,128)} %param.7) | copy-start | bytes 393220
  263.8 200.4 %all-gather.8.cloned.1.call-start = ((), (), s32[]{:S(2)}) async-start(), calls=%async_computation.10 | async-start | bytes 1179648 | tf_op jit(solution)/shard_map/all_gather | solution.py:85
  265.9 0.7 copy-start.12
  265.9 0.7 copy-start.13
  474.7 20.7 %all-to-all-start.4 = ((f32[64,1,1024]{2,1,0:T(1,128)}), f32[64,1,1024]{2,1,0:T(1,128)S(1)}, u32[]{:S(2)}, u32[]{:S(2)}) async-start(f32[64,1,1024]{2,1,0:T(1,128)} %reshape.1074), calls=%async_computation.4 | async-start | bytes 524288 | tf_op jit(solution)/shard_map/all_to_all | solution.py:92
  495.5 17.7 %all-to-all-start.6 = ((f32[64,1,1024]{2,1,0:T(1,128)}), f32[64,1,1024]{2,1,0:T(1,128)S(1)}, u32[]{:S(2)}, u32[]{:S(2)}) async-start(f32[64,1,1024]{2,1,0:T(1,128)} %reshape.1070), calls=%async_computation.6 | async-start | bytes 524288 | tf_op jit(solution)/shard_map/all_to_all | solution.py:92
  516.2 0.9 copy-start.6
  520.1 1.0 copy-start.4
  526.1 17.7 %all-to-all-start.5 = ((f32[64,1,1024]{2,1,0:T(1,128)}), f32[64,1,1024]{2,1,0:T(1,128)S(1)}, u32[]{:S(2)}, u32[]{:S(2)}) async-start(f32[64,1,1024]{2,1,0:T(1,128)} %reshape.1076), calls=%async_computation.5 | async-start | bytes 524288 | tf_op jit(solution)/shard_map/all_to_all | solution.py:95
  543.8 17.7 %all-to-all-start.7 = ((f32[64,1,1024]{2,1,0:T(1,128)}), f32[64,1,1024]{2,1,0:T(1,128)S(1)}, u32[]{:S(2)}, u32[]{:S(2)}) async-start(f32[64,1,1024]{2,1,0:T(1,128)} %reshape.1072), calls=%async_computation.7 | async-start | bytes 524288 | tf_op jit(solution)/shard_map/all_to_all | solution.py:95
  550.1 155.7 %all-reduce.7.cloned.1.call-start = ((), (), s32[]{:S(2)}) async-start(), calls=%async_computation.12 | async-start | bytes 2097152
  570.3 135.5 %copy-start.1 = (f32[32,1,2,2,256]{4,3,2,1,0:T(2,128)S(1)}, f32[32,1,2,2,256]{4,3,2,1,0:T(2,128)}, u32[]{:S(2)}) copy-start(f32[32,1,2,2,256]{4,3,2,1,0:T(2,128)} %dynamic-slice_add_fusion.1) | copy-start | bytes 393220
Sparse Core Ops, SparseCore 0:
  11.2 70.1 all-gather.5
  85.2 63.1 all-gather.3
  263.9 135.2 all-reduce.4
  402.8 61.2 all-gather.7
  570.4 135.3 all-reduce.6
where the time goes:
time: 723 us; the launch traced here: 714 us
  waiting for transfers between devices  518 us (72%)
  matrix products  59.5 us (8%)
  starting transfers between devices  59.1 us (8%)
  local copies, waits for them, and re-layouts  33.3 us (5%)
  other arithmetic  28.5 us (4%)
  between operations  15.6 us (2%)
    unnamed x7, waiting for transfers between devices  269 us
    all_gather x2, waiting for transfers between devices, apply(): whole = lax.all_gather(state, 'rows', axis=0, tiled=True)  128 us
    all_gather x1, waiting for transfers between devices, per_device(): points_all = lax.all_gather(valence_values, 'rows', axis=1, tiled=True)  68.8 us
    dot_general x84, matrix products, product(): return jnp.einsum(formula, left, right, precision=lax.Precision.HIGHEST)  59.5 us
    all_to_all x4, starting transfers between devices, apply(): lax.all_to_all(expand(chosen, valence_couple), 'ka', split_axis=3, concat...  32.3 us
    all_to_all x4, waiting for transfers between devices, apply(): lax.all_to_all(spectral(sent, weights, forward), 'ka', split_axis=2, conc...  32.3 us
    all_to_all x4, starting transfers between devices, apply(): lax.all_to_all(spectral(sent, weights, forward), 'ka', split_axis=2, conc...  26.3 us
    all_to_all x4, waiting for transfers between devices, apply(): lax.all_to_all(expand(chosen, valence_couple), 'ka', split_axis=3, concat...  20.3 us
  transfers between devices with their start and end apart: 13, of which 13 were waited for; matrix products, arithmetic and copies ran while one was open for 6% of the time, Pallas kernels for 0%

commit v1 on v0

v1 whole, which is shorter than its diff:
```python
import jax
import jax.numpy as jnp
from jax import lax
from jax.experimental import pallas as pl
from jax.experimental.pallas import tpu as pltpu
from jax.sharding import Mesh, PartitionSpec as P


KA = ("zl", "y", "core")
ROWS = ("x", "zh")
F32, BF16 = jnp.float32, jnp.bfloat16
VMEM = pl.BlockSpec(memory_space=pltpu.VMEM)
SMEM = pl.BlockSpec(memory_space=pltpu.SMEM)

PARAMS = pltpu.CompilerParams(vmem_limit_bytes=20 * 2**20)

NN = (((1,), (0,)), ((), ()))
NT = (((1,), (1,)), ((), ()))


def shape(dims, dtype=F32):
    return jax.ShapeDtypeStruct(dims, dtype)


def split(value):
    high = value.astype(BF16)
    return high, (value - high.astype(F32)).astype(BF16)


def dot3(left, right, dims):
    def one(a, b):
        return lax.dot_general(a, b, dims, preferred_element_type=F32)

    return one(left[0], right[0]) + (one(left[0], right[1]) + one(left[1], right[0]))


def complex_pair(real, imag):
    return jnp.concatenate(
        [jnp.concatenate([real, imag], axis=1), jnp.concatenate([-imag, real], axis=1)], axis=0
    )


def with_turned(mixed):
    half = mixed.shape[1] // 2
    turned = jnp.concatenate([mixed[:, half:], -mixed[:, :half]], axis=1)
    return split(jnp.concatenate([mixed, turned], axis=0))


def transposed(ref):
    half = ref.shape[1] // 2
    return jnp.concatenate([ref[:, :half].T, ref[:, half:].T], axis=1)


def multiply_out(real, imag, pc_h, pc_l, qc_h, qc_l, out):
    mixed = dot3((pc_h[...], pc_l[...]), split(complex_pair(real, imag)), NN)
    pairs = dot3((qc_h[...], qc_l[...]), with_turned(mixed), NT)
    out[:, 0:8, :] = pairs[:, :128].reshape(64, 8, 128)
    out[:, 8:16, :] = pairs[:, 128:].reshape(64, 8, 128)


def first_kernel(zh, own, par, p_own, p_par, pc_h, pc_l, qc_h, qc_l, out):
    mine = zh[0]
    real, imag = [], []
    for x in range(4):
        for h in range(2):
            rows = pl.ds((2 * x + h) * 64, 64)
            for part in range(2):
                source = pl.ds(part * 64, 64)
                piece = jnp.where(mine == h, own[x, source, :], par[x, source, :])
                high, low = split(piece)
                qc_h[rows, pl.ds(part * 256, 256)] = high
                qc_l[rows, pl.ds(part * 256, 256)] = low
                source = pl.ds(128 + part * 32, 32)
                piece = jnp.where(mine == h, own[x, source, :], par[x, source, :])
                (imag if part else real).append(piece)
    for h in range(2):
        for part in range(2):
            source = pl.ds(part * 64, 64)
            piece = jnp.where(mine == h, p_own[source, :], p_par[source, :])
            high, low = split(piece)
            pc_h[pl.ds(h * 64, 64), pl.ds(part * 256, 256)] = high
            pc_l[pl.ds(h * 64, 64), pl.ds(part * 256, 256)] = low
    real, imag = jnp.concatenate(real, axis=0), jnp.concatenate(imag, axis=0)
    multiply_out(real, imag, pc_h, pc_l, qc_h, qc_l, out)


def first(zh, own, par, p_own, p_par):
    return pl.pallas_call(
        first_kernel,
        out_shape=(
            shape((128, 512), BF16),
            shape((128, 512), BF16),
            shape((512, 512), BF16),
            shape((512, 512), BF16),
            shape((64, 16, 128)),
        ),
        in_specs=[SMEM] + [VMEM] * 4,
        out_specs=(VMEM,) * 5,
        name="first",
        compiler_params=PARAMS,
    )(zh, own, par, p_own, p_par)


def forward_kernel(state, pc_h, pc_l, qc_h, qc_l, out):
    real = jnp.concatenate([state[x, h, 0] for x in range(4) for h in range(2)], axis=0)
    imag = jnp.concatenate([state[x, h, 1] for x in range(4) for h in range(2)], axis=0)
    multiply_out(real, imag, pc_h, pc_l, qc_h, qc_l, out)


def forward(state, pc, qc):
    return pl.pallas_call(
        forward_kernel,
        out_shape=shape((64, 16, 128)),
        in_specs=[VMEM] * 5,
        out_specs=VMEM,
        name="forward",
        compiler_params=PARAMS,
    )(state, *pc, *qc)


def backward_kernel(block, pc_h, pc_l, qc_h, qc_l, out):
    real = block[:, 0:8, :].reshape(512, 128)
    imag = block[:, 8:16, :].reshape(512, 128)
    valence = (transposed(qc_h), transposed(qc_l))
    mixed = dot3(valence, split(complex_pair(real, imag)), NN)
    conduction = (transposed(pc_h), transposed(pc_l))
    term = dot3(conduction, with_turned(mixed), NT)
    for row in range(8):
        out[row, 0] = term[row * 32 : row * 32 + 32, :256]
        out[row, 1] = term[row * 32 : row * 32 + 32, 256:]


def backward(block, pc, qc):
    return pl.pallas_call(
        backward_kernel,
        out_shape=shape((8, 2, 32, 256)),
        in_specs=[VMEM] * 5,
        out_specs=VMEM,
        name="backward",
        compiler_params=PARAMS,
    )(block, *pc, *qc)


def once_kernel(zh, keep, got, out):
    mine = zh[0]
    for part in range(2):
        low = jnp.where(mine == 0, keep[part], got[part])
        high = jnp.where(mine == 0, got[part], keep[part])
        out[:, 0, part] = jnp.stack([low, high], axis=1)


def place_once(zh, keep, got):
    return pl.pallas_call(
        once_kernel,
        out_shape=shape((32, 1, 2, 2, 256)),
        in_specs=[SMEM, VMEM, VMEM],
        out_specs=VMEM,
        name="place_once",
        compiler_params=PARAMS,
    )(zh, keep, got)


def twice_kernel(once, energy, parts, out):
    for part in range(2):
        terms = []
        for vector in range(2):
            rows = [parts[2 * x + vector, pl.ds(32 * part, 32), :] for x in range(4)]
            terms.append((rows[0] + rows[1]) + (rows[2] + rows[3]))
        factor = energy[...]
        factor = jnp.stack([factor, factor], axis=1)
        out[:, 0, part] = factor * once[:, 0, part] + jnp.stack(terms, axis=1)


def place_twice(once, energy, parts):
    return pl.pallas_call(
        twice_kernel,
        out_shape=shape((32, 1, 2, 2, 256)),
        in_specs=[VMEM] * 3,
        out_specs=VMEM,
        name="place_twice",
        compiler_params=PARAMS,
    )(once, energy, parts)


def butterfly(values, sign):
    (r0, i0), (r1, i1), (r2, i2), (r3, i3) = values
    ar, ai, br, bi = r0 + r2, i0 + i2, r0 - r2, i0 - i2
    cr, ci, dr, di = r1 + r3, i1 + i3, r1 - r3, i1 - i3
    plus, minus = (br - di, bi + dr), (br + di, bi - dr)
    first, last = (minus, plus) if sign < 0 else (plus, minus)
    return [(ar + cr, ai + ci), first, (ar - cr, ai - ci), last]


def plane(values, sign):
    for row in range(4):
        values[4 * row : 4 * row + 4] = butterfly(values[4 * row : 4 * row + 4], sign)
    for column in range(4):
        values[column::4] = butterfly(values[column::4], sign)
    return values


def read(ref, index):
    return ref[index, 0:8, :], ref[index, 8:16, :]


def write(ref, index, value):
    ref[index, 0:8, :], ref[index, 8:16, :] = value


def weights_kernel(zh, own, par, out):
    mine = zh[0]
    lane = lax.broadcasted_iota(jnp.int32, (8, 128), 1)
    for a in range(4):
        values = []
        for f in range(16 * a, 16 * a + 16):
            rows = pl.ds(f % 32 * 8, 8)
            columns = pl.ds(f // 32 * 128, 128)
            there = par[pl.ds(128 + f % 32 * 8, 8), columns]
            here = own[rows, columns]
            low = jnp.where(mine == 0, here, there)
            high = jnp.where(mine == 0, there, here)
            real = jnp.where(lane < 64, low, pltpu.roll(high, 64, 1)) * (1.0 / 64)
            imag = jnp.where(lane < 64, pltpu.roll(low, 64, 1), high) * (1.0 / 64)
            values.append((real, imag))
        for f, value in enumerate(plane(values, -1)):
            write(out, 16 * a + f, value)
    for f in range(16):
        values = butterfly([read(out, 16 * a + f) for a in range(4)], -1)
        for a in range(4):
            write(out, 16 * a + f, values[a])


def transform_weights(zh, own, par):
    return pl.pallas_call(
        weights_kernel,
        out_shape=shape((64, 16, 128)),
        in_specs=[SMEM, VMEM, VMEM],
        out_specs=VMEM,
        name="weights",
        compiler_params=PARAMS,
    )(zh, own, par)


def spectral_kernel(place, block, weight, out, work):
    for a in range(4):
        values = [read(block, place[16 * a + f]) for f in range(16)]
        for f, value in enumerate(plane(values, -1)):
            write(work, 16 * a + f, value)
    for f in range(16):
        values = butterfly([read(work, 16 * a + f) for a in range(4)], -1)
        scaled = []
        for a in range(4):
            (r, i), (wr, wi) = values[a], read(weight, 16 * a + f)
            scaled.append((wr * r - wi * i, wr * i + wi * r))
        values = butterfly(scaled, 1)
        for a in range(4):
            write(work, 16 * a + f, values[a])
    for a in range(4):
        values = plane([read(work, 16 * a + f) for f in range(16)], 1)
        for f in range(16):
            write(out, place[16 * a + f], values[f])


def spectral(place, block, weight):
    return pl.pallas_call(
        spectral_kernel,
        out_shape=shape((64, 16, 128)),
        in_specs=[SMEM, VMEM, VMEM],
        out_specs=VMEM,
        scratch_shapes=[pltpu.VMEM((64, 16, 128), F32)],
        name="spectral",
        compiler_params=PARAMS,
    )(place, block, weight)


def exchange(value, axes):
    return lax.all_to_all(value, axes, split_axis=0, concat_axis=0, tiled=True)


def gather_x(value):
    return exchange(jnp.broadcast_to(value[None], (4,) + value.shape), "x")


def swap(value):
    return lax.ppermute(value, "zh", [(0, 1), (1, 0)])


def per_device(
    amplitudes,
    conduction_values,
    valence_values,
    screened,
    conduction_energy,
    valence_energy,
    offset_table,
):
    zh = lax.axis_index("zh").astype(jnp.int32)
    first_half = zh == 0
    zh_scalar = zh[None]

    grid = offset_table[:, 0]
    points = jnp.arange(64, dtype=jnp.int32)
    place = jnp.sum(jnp.where(grid[None, :] == points[:, None], points[None, :], 0), axis=1)

    state = amplitudes[:, 0]
    s0 = state[:, :, 0].transpose(1, 0, 2).reshape(64, 256)
    s1 = state[:, :, 1].transpose(1, 0, 2).reshape(64, 256)
    keep = jnp.where(first_half, s0, s1)
    give = jnp.where(first_half, s1, s0)
    cond_row = jnp.pad(conduction_energy.reshape(1, 32), ((0, 7), (0, 224)))
    q_own = valence_values.reshape(128, 256)
    p_own = conduction_values.reshape(128, 256)
    par1 = swap(jnp.concatenate([q_own, give, cond_row], axis=0))
    w_own = jnp.concatenate(
        [screened[part, 32 * at : 32 * at + 32] for at in range(2) for part in range(2)], axis=-1
    ).reshape(256, 256)
    par2 = swap(jnp.concatenate([p_own, w_own], axis=0))

    own4 = gather_x(jnp.concatenate([q_own, keep], axis=0))
    par4 = gather_x(par1[:192])

    def ordered(own, par, axis):
        return jnp.where(
            first_half, jnp.stack([own, par], axis=axis), jnp.stack([par, own], axis=axis)
        )

    own_cond = conduction_energy[:, 0]
    par_cond = par1[192, :32]
    energy = (ordered(own_cond, par_cond, 0)[:, :, None] - valence_energy[0][None, None])[:, None]
    own_energy = own_cond[:, None] - valence_energy[0][None]
    state_q = ordered(keep.reshape(2, 32, 256), par1[128:192].reshape(2, 32, 256), 0)

    weight = transform_weights(zh_scalar, w_own, par2)
    own4, par4, weight, place, energy, own_energy, state_q = lax.optimization_barrier(
        (own4, par4, weight, place, energy, own_energy, state_q)
    )
    pc_h, pc_l, qc_h, qc_l, pairs = first(zh_scalar, own4, par4, p_own, par2)
    pc, qc = (pc_h, pc_l), (qc_h, qc_l)

    def convolve(block):
        sent = exchange(block, KA)
        back = exchange(spectral(place, sent, weight), KA)
        return backward(back, pc, qc)

    parts = exchange(convolve(pairs).reshape(4, 128, 256), "x")
    parts = parts.reshape(4, 2, 2, 32, 256)
    state_q = energy * state_q + jnp.sum(parts, axis=0)
    state_all = gather_x(state_q)

    keep = jnp.where(first_half, state_q[0], state_q[1])
    give = jnp.where(first_half, state_q[1], state_q[0])
    got = swap(give.reshape(64, 256)).reshape(2, 32, 256)
    once = place_once(zh_scalar, keep, got)

    pairs = forward(state_all, pc, qc)
    parts = exchange(convolve(pairs).reshape(8, 64, 256), ROWS)
    return once, place_twice(once, own_energy, parts)


def solution(mesh):
    fine = Mesh(mesh.devices.reshape(4, 8, 2, 4, 2), KA + ROWS)
    specs = (
        P(ROWS, KA, None, None, None),
        P(None, ROWS, KA, None),
        P(None, ROWS, KA, None),
        P(None, None, KA, ROWS),
        P(ROWS, KA),
        P(KA, None),
        P(),
    )

    return jax.shard_map(
        per_device,
        mesh=fine,
        in_specs=specs,
        out_specs=(P(ROWS, KA, None, None, None),) * 2,
        check_vma=False,
    )
```

time: 723 us -> 204 us (0.28)
  the two profiles are of different devices: /device:TPU:72 before, /device:TPU:8 now
where the time goes in v1:
time: 204 us; the launch traced here: 203 us
  blocking collectives  122 us (60%)
  starting transfers between devices  32 us (16%)
  waiting for transfers between devices  27.4 us (13%)
  local copies, waits for them, and re-layouts  9.32 us (5%)
  Pallas kernels  9.09 us (4%)
  other arithmetic  2.61 us (1%)
    all_to_all x6, blocking collectives, exchange(): return lax.all_to_all(value, axes, split_axis=0, concat_axis=0, tiled=True)  122 us
    ppermute x3, starting transfers between devices, swap(): return lax.ppermute(value, 'zh', [(0, 1), (1, 0)])  20.6 us
    all_to_all x3, waiting for transfers between devices, exchange(): return lax.all_to_all(value, axes, split_axis=0, concat_axis=0, tiled=True)  15.3 us
    ppermute x3, waiting for transfers between devices, swap(): return lax.ppermute(value, 'zh', [(0, 1), (1, 0)])  12.1 us
    all_to_all x3, starting transfers between devices, exchange(): return lax.all_to_all(value, axes, split_axis=0, concat_axis=0, tiled=True)  11.4 us
    unnamed x39, local copies, waits for them, and re-layouts  6.4 us
  transfers between devices with their start and end apart: 6, of which 3 were waited for; matrix products, arithmetic and copies ran while one was open for 2% of the time, Pallas kernels for 0%

profile of v1, /device:TPU:8, one launch (start us, length us, event | category | flops | bytes accessed | tf_op | source)
XLA Modules:
  0.0 203.0 jit_solution(13761955646632904139)
XLA Ops:
  0.6 1.0 copy.15
  2.3 10.9 %collective-permute-start = (f32[200,256]{1,0:T(8,128)S(1)}, f32[200,256]{1,0:T(8,128)S(1)}, u32[]{:S(2)}, u32[]{:S(2)}) collective-permute-start(f32[200,256]{1,0:T(8,128)S(1)} %select_maximum_fusion), channel_id=1, source_target_pairs={{0,1},{1,0},{2,3},{3,2},{4,5},{5,4},{6,7},{7,6},{8,9},{9,8},{10,11... | collective-permute-start | bytes 614408 | tf_op jit(solution)/shard_map/ppermute | solution.py:285
  13.3 0.9 broadcast_in_dim.21
  14.2 4.4 %all-to-all-start = ((f32[4,192,256]{2,1,0:T(8,128)}), f32[4,192,256]{2,1,0:T(8,128)S(1)}, u32[]{:S(2)}, u32[]{:S(2)}) async-start(f32[4,192,256]{2,1,0:T(8,128)} %broadcast_in_dim.21), calls=%async_computation | async-start | bytes 1572864 | tf_op jit(solution)/shard_map/all_to_all | solution.py:277
  19.5 1.9 collective-permute-start.1
  23.0 7.7 %all-to-all-done.own = f32[4,192,256]{2,1,0:T(8,128)S(1)} async-done(((f32[4,192,256]{2,1,0:T(8,128)}), f32[4,192,256]{2,1,0:T(8,128)S(1)}, u32[]{:S(2)}, u32[]{:S(2)}) %all-to-all-start) | async-done | bytes 786464 | tf_op jit(solution)/shard_map/all_to_all | solution.py:277
  30.7 0.9 broadcast_in_dim.22
  31.6 3.5 %all-to-all-start.1 = ((f32[4,192,256]{2,1,0:T(8,128)}), f32[4,192,256]{2,1,0:T(8,128)S(1)}, u32[]{:S(2)}, u32[]{:S(2)}) async-start(f32[4,192,256]{2,1,0:T(8,128)} %broadcast_in_dim.22), calls=%async_computation.1 | async-start | bytes 1572864 | tf_op jit(solution)/shard_map/all_to_all | solution.py:277
  35.4 0.8 copy-done.11
  36.2 0.8 slice-done
  37.7 0.7 broadcast_subtract_fusion
  38.6 7.6 %all-to-all-done.1.par = f32[4,192,256]{2,1,0:T(8,128)S(1)} async-done(((f32[4,192,256]{2,1,0:T(8,128)}), f32[4,192,256]{2,1,0:T(8,128)S(1)}, u32[]{:S(2)}, u32[]{:S(2)}) %all-to-all-start.1) | async-done | bytes 786464 | tf_op jit(solution)/shard_map/all_to_all | solution.py:277
  46.2 0.9 copy-done.5
  47.1 1.1 first.1
  48.2 28.3 %all_to_all.45.block = f32[64,16,128]{2,1,0:T(8,128)S(1)} all-to-all(f32[64,16,128]{2,1,0:T(8,128)S(1)} %get-tuple-element.19), channel_id=1, replica_groups=mesh['zl'=4,'y'=8,'core'=2,'x'=4,'zh'=2] {'zl','y','core'}, dimensions={0} | all-to-all | bytes 1048576 | tf_op jit(solution)/shard_map/all_to_all | solution.py:277
  76.5 0.9 spectral.2
  77.4 23.1 %all_to_all.46.block = f32[64,16,128]{2,1,0:T(8,128)S(1)} all-to-all(f32[64,16,128]{2,1,0:T(8,128)S(1)} %spectral.2), channel_id=1, replica_groups=mesh['zl'=4,'y'=8,'core'=2,'x'=4,'zh'=2] {'zl','y','core'}, dimensions={0} | all-to-all | bytes 1048576 | tf_op jit(solution)/shard_map/all_to_all | solution.py:277
  100.5 1.3 backward.2
  101.8 11.6 %all_to_all.47 = f32[4,128,256]{2,1,0:T(8,128)S(1)} all-to-all(f32[4,128,256]{2,1,0:T(8,128)S(1)} %bitcast.38), channel_id=1, replica_groups=mesh['zl'=4,'y'=8,'core'=2,'x'=4,'zh'=2] {'x'}, dimensions={0} | all-to-all | bytes 1048576 | tf_op jit(solution)/shard_map/all_to_all | solution.py:277
  113.5 0.9 copy-done.8
  114.4 10.9 %all_to_all.48.state = f32[4,2,2,32,256]{4,3,2,1,0:T(8,128)S(1)} all-to-all(f32[4,2,2,32,256]{4,3,2,1,0:T(8,128)S(1)} %broadcast_in_dim.42), channel_id=1, replica_groups=mesh['zl'=4,'y'=8,'core'=2,'x'=4,'zh'=2] {'x'}, dimensions={0} | all-to-all | bytes 1048576 | tf_op jit(solution)/shard_map/all_to_all | solution.py:277
  125.4 1.0 forward.1
  126.4 24.7 %all_to_all.49.block = f32[64,16,128]{2,1,0:T(8,128)S(1)} all-to-all(f32[64,16,128]{2,1,0:T(8,128)S(1)} %forward.1), channel_id=1, replica_groups=mesh['zl'=4,'y'=8,'core'=2,'x'=4,'zh'=2] {'zl','y','core'}, dimensions={0} | all-to-all | bytes 1048576 | tf_op jit(solution)/shard_map/all_to_all | solution.py:277
  151.1 0.9 spectral.3
  151.9 23.1 %all_to_all.50.block = f32[64,16,128]{2,1,0:T(8,128)S(1)} all-to-all(f32[64,16,128]{2,1,0:T(8,128)S(1)} %spectral.3), channel_id=1, replica_groups=mesh['zl'=4,'y'=8,'core'=2,'x'=4,'zh'=2] {'zl','y','core'}, dimensions={0} | all-to-all | bytes 1048576 | tf_op jit(solution)/shard_map/all_to_all | solution.py:277
  175.0 2.1 %backward.3 = f32[8,2,32,256]{3,2,1,0:T(8,128)} custom-call(f32[64,16,128]{2,1,0:T(8,128)S(1)} %all_to_all.50.block, bf16[128,512]{1,0:T(8,128)(2,1)S(1)} %copy-done.1, bf16[128,512]{1,0:T(8,128)(2,1)S(1)} %copy-done.3, bf16[512,512]{1,0:T(8,128)(2,1)S(1)} %get-tuple-element.23.qc_h, bf16[512,512]{1,0:T(8,128)(2,1)S(1)} %get-tuple-element.24.qc_l), custom_call_target="tpu_custom_call" | custom-call | tf_op jit(solution)/shard_map/backward/pallas_call | solution.py:134
  177.1 3.5 %all-to-all-start.8 = ((f32[8,64,256]{2,1,0:T(8,128)}), f32[8,64,256]{2,1,0:T(8,128)S(1)}, u32[]{:S(2)}, u32[]{:S(2)}) async-start(f32[8,64,256]{2,1,0:T(8,128)} %bitcast.25), calls=%async_computation.8 | async-start | bytes 1048576 | tf_op jit(solution)/shard_map/all_to_all | solution.py:277
  180.7 7.7 %collective-permute-start.2 = (f32[64,256]{1,0:T(8,128)S(1)}, f32[64,256]{1,0:T(8,128)S(1)}, u32[]{:S(2)}, u32[]{:S(2)}) collective-permute-start(f32[64,256]{1,0:T(8,128)S(1)} %bitcast.51), channel_id=1, source_target_pairs={{0,1},{1,0},{2,3},{3,2},{4,5},{5,4},{6,7},{7,6},{8,9},{9,8},{10,11... | collective-permute-start | bytes 196616 | tf_op jit(solution)/shard_map/ppermute | solution.py:285
  188.4 12.1 %collective-permute-done.2 = f32[64,256]{1,0:T(8,128)S(1)} collective-permute-done((f32[64,256]{1,0:T(8,128)S(1)}, f32[64,256]{1,0:T(8,128)S(1)}, u32[]{:S(2)}, u32[]{:S(2)}) %collective-permute-start.2) | collective-permute-done | bytes 65568 | tf_op jit(solution)/shard_map/ppermute | solution.py:285
  200.5 0.8 place_once.1.once
  201.3 0.9 copy-done.6
  202.2 0.8 place_twice.1
  (56 shorter events, 4.4 us)
Async XLA Ops:
  0.6 1.0 copy-start.13
  1.7 0.7 copy-start.16
  2.3 20.6 %collective-permute-start = (f32[200,256]{1,0:T(8,128)S(1)}, f32[200,256]{1,0:T(8,128)S(1)}, u32[]{:S(2)}, u32[]{:S(2)}) collective-permute-start(f32[200,256]{1,0:T(8,128)S(1)} %select_maximum_fusion), channel_id=1, source_target_pairs={{0,1},{1,0},{2,3},{3,2},{4,5},{5,4},{6,7},{7,6},{8,9},{9,8},{10,11... | collective-permute-start | bytes 614408 | tf_op jit(solution)/shard_map/ppermute | solution.py:285
  14.2 4.4 %copy-start.14 = (f32[2,64,1,256]{3,2,1,0:T(1,128)S(1)}, f32[2,64,1,256]{3,2,1,0:T(1,128)}, u32[]{:S(2)}) copy-start(f32[2,64,1,256]{3,2,1,0:T(1,128)} %param.8) | copy-start | bytes 393220
  14.2 4.4 %copy-start.9 = (f32[2,64,8,64]{3,2,1,0:T(8,128)S(1)}, f32[2,64,8,64]{3,2,1,0:T(8,128)}, u32[]{:S(2)}) copy-start(f32[2,64,8,64]{3,2,1,0:T(8,128)} %param.10) | copy-start | bytes 786436
  14.2 16.4 %all-to-all-start = ((f32[4,192,256]{2,1,0:T(8,128)}), f32[4,192,256]{2,1,0:T(8,128)S(1)}, u32[]{:S(2)}, u32[]{:S(2)}) async-start(f32[4,192,256]{2,1,0:T(8,128)} %broadcast_in_dim.21), calls=%async_computation | async-start | bytes 1572864 | tf_op jit(solution)/shard_map/all_to_all | solution.py:277
  18.7 0.7 copy-start.4
  19.3 2.1 %copy-start.15 = (s32[64,64]{1,0:T(8,128)S(1)}, s32[64,64]{1,0:T(8,128)}, u32[]{:S(2)}) copy-start(s32[64,64]{1,0:T(8,128)} %param.13) | copy-start | bytes 49156
  19.5 18.9 %collective-permute-start.1 = (f32[384,256]{1,0:T(8,128)S(1)}, f32[384,256]{1,0:T(8,128)S(1)}, u32[]{:S(2)}, u32[]{:S(2)}) collective-permute-start(f32[384,256]{1,0:T(8,128)S(1)} %maximum_maximum_fusion), channel_id=1, source_target_pairs={{0,1},{1,0},{2,3},{3,2},{4,5},{5,4},{6,7},{7,6},{8,9},{9,8},{10,11... | collective-permute-start | bytes 1179656 | tf_op jit(solution)/shard_map/ppermute | solution.py:285
  21.6 0.7 copy-start.17
  22.9 8.7 %copy-start.10 = (f32[200,256]{1,0:T(8,128)}, f32[200,256]{1,0:T(8,128)S(1)}, u32[]{:S(2)}) copy-start(f32[200,256]{1,0:T(8,128)S(1)} %collective-permute-done) | copy-start | bytes 614404
  31.6 14.6 %all-to-all-start.1 = ((f32[4,192,256]{2,1,0:T(8,128)}), f32[4,192,256]{2,1,0:T(8,128)S(1)}, u32[]{:S(2)}, u32[]{:S(2)}) async-start(f32[4,192,256]{2,1,0:T(8,128)} %broadcast_in_dim.22), calls=%async_computation.1 | async-start | bytes 1572864 | tf_op jit(solution)/shard_map/all_to_all | solution.py:277
  35.2 0.9 copy-start.11
  36.2 0.8 slice-start
  46.2 0.9 copy-start.5
  48.2 52.3 %copy-start = (bf16[128,512]{1,0:T(8,128)(2,1)}, bf16[128,512]{1,0:T(8,128)(2,1)S(1)}, u32[]{:S(2)}) copy-start(bf16[128,512]{1,0:T(8,128)(2,1)S(1)} %get-tuple-element.21.pc_h) | copy-start | bytes 393220
  48.2 52.3 %copy-start.2 = (bf16[128,512]{1,0:T(8,128)(2,1)}, bf16[128,512]{1,0:T(8,128)(2,1)S(1)}, u32[]{:S(2)}) copy-start(bf16[128,512]{1,0:T(8,128)(2,1)S(1)} %get-tuple-element.22.pc_l) | copy-start | bytes 393220
  113.4 0.9 copy-start.8
  113.4 0.9 copy-start.12
  114.4 10.9 %copy-start.1 = (bf16[128,512]{1,0:T(8,128)(2,1)S(1)}, bf16[128,512]{1,0:T(8,128)(2,1)}, u32[]{:S(2)}) copy-start(bf16[128,512]{1,0:T(8,128)(2,1)} %copy-done) | copy-start | bytes 393220
  114.4 10.9 %copy-start.3 = (bf16[128,512]{1,0:T(8,128)(2,1)S(1)}, bf16[128,512]{1,0:T(8,128)(2,1)}, u32[]{:S(2)}) copy-start(bf16[128,512]{1,0:T(8,128)(2,1)} %copy-done.2) | copy-start | bytes 393220
  177.1 24.1 %all-to-all-start.8 = ((f32[8,64,256]{2,1,0:T(8,128)}), f32[8,64,256]{2,1,0:T(8,128)S(1)}, u32[]{:S(2)}, u32[]{:S(2)}) async-start(f32[8,64,256]{2,1,0:T(8,128)} %bitcast.25), calls=%async_computation.8 | async-start | bytes 1048576 | tf_op jit(solution)/shard_map/all_to_all | solution.py:277
  180.7 19.9 %collective-permute-start.2 = (f32[64,256]{1,0:T(8,128)S(1)}, f32[64,256]{1,0:T(8,128)S(1)}, u32[]{:S(2)}, u32[]{:S(2)}) collective-permute-start(f32[64,256]{1,0:T(8,128)S(1)} %bitcast.51), channel_id=1, source_target_pairs={{0,1},{1,0},{2,3},{3,2},{4,5},{5,4},{6,7},{7,6},{8,9},{9,8},{10,11... | collective-permute-start | bytes 196616 | tf_op jit(solution)/shard_map/ppermute | solution.py:285
  200.5 0.8 copy-start.7
  201.3 0.9 copy-start.6

commit v2 on v1

--- a/solution.py
+++ b/solution.py
@@ -141,45 +141,59 @@
     )(block, *pc, *qc)
 
 
-def once_kernel(zh, keep, got, out):
+def update_kernel(zh, state, energy, parts, out, keep, give):
     mine = zh[0]
+    values = []
+    for h in range(2):
+        for part in range(2):
+            rows = [parts[x, pl.ds(64 * h + 32 * part, 32), :] for x in range(4)]
+            term = (rows[0] + rows[1]) + (rows[2] + rows[3])
+            value = energy[h] * state[h, part] + term
+            for x in range(4):
+                out[x, h, part] = value
+            values.append(value)
     for part in range(2):
-        low = jnp.where(mine == 0, keep[part], got[part])
-        high = jnp.where(mine == 0, got[part], keep[part])
-        out[:, 0, part] = jnp.stack([low, high], axis=1)
-
-
-def place_once(zh, keep, got):
-    return pl.pallas_call(
-        once_kernel,
-        out_shape=shape((32, 1, 2, 2, 256)),
-        in_specs=[SMEM, VMEM, VMEM],
-        out_specs=VMEM,
-        name="place_once",
-        compiler_params=PARAMS,
-    )(zh, keep, got)
-
-
-def twice_kernel(once, energy, parts, out):
+        keep[part] = jnp.where(mine == 0, values[part], values[2 + part])
+        give[pl.ds(32 * part, 32), :] = jnp.where(mine == 0, values[2 + part], values[part])
+
+
+def update(zh, state, energy, parts):
+    return pl.pallas_call(
+        update_kernel,
+        out_shape=(shape((4, 2, 2, 32, 256)), shape((2, 32, 256)), shape((64, 256))),
+        in_specs=[SMEM] + [VMEM] * 3,
+        out_specs=(VMEM,) * 3,
+        name="update",
+        compiler_params=PARAMS,
+    )(zh, state, energy, parts)
+
+
+def finish_kernel(zh, keep, got, energy, parts, once, twice):
+    mine = zh[0]
+    factor = energy[...]
+    factor = jnp.stack([factor, factor], axis=1)
     for part in range(2):
+        here, there = keep[part], got[pl.ds(32 * part, 32), :]
+        low = jnp.where(mine == 0, here, there)
+        high = jnp.where(mine == 0, there, here)
+        before = jnp.stack([low, high], axis=1)
         terms = []
         for vector in range(2):
             rows = [parts[2 * x + vector, pl.ds(32 * part, 32), :] for x in range(4)]
             terms.append((rows[0] + rows[1]) + (rows[2] + rows[3]))
-        factor = energy[...]
-        factor = jnp.stack([factor, factor], axis=1)
-        out[:, 0, part] = factor * once[:, 0, part] + jnp.stack(terms, axis=1)
-
-
-def place_twice(once, energy, parts):
-    return pl.pallas_call(
-        twice_kernel,
-        out_shape=shape((32, 1, 2, 2, 256)),
-        in_specs=[VMEM] * 3,
-        out_specs=VMEM,
-        name="place_twice",
-        compiler_params=PARAMS,
-    )(once, energy, parts)
+        once[:, 0, part] = before
+        twice[:, 0, part] = factor * before + jnp.stack(terms, axis=1)
+
+
+def finish(zh, keep, got, energy, parts):
+    return pl.pallas_call(
+        finish_kernel,
+        out_shape=(shape((32, 1, 2, 2, 256)),) * 2,
+        in_specs=[SMEM] + [VMEM] * 4,
+        out_specs=(VMEM,) * 2,
+        name="finish",
+        compiler_params=PARAMS,
+    )(zh, keep, got, energy, parts)
 
 
 def butterfly(values, sign):
@@ -216,7 +230,7 @@
             rows = pl.ds(f % 32 * 8, 8)
             columns = pl.ds(f // 32 * 128, 128)
             there = par[pl.ds(128 + f % 32 * 8, 8), columns]
-            here = own[rows, columns]
+            here = own[pl.ds(128 + f % 32 * 8, 8), columns]
             low = jnp.where(mine == 0, here, there)
             high = jnp.where(mine == 0, there, here)
             real = jnp.where(lane < 64, low, pltpu.roll(high, 64, 1)) * (1.0 / 64)
@@ -307,34 +321,33 @@
     s1 = state[:, :, 1].transpose(1, 0, 2).reshape(64, 256)
     keep = jnp.where(first_half, s0, s1)
     give = jnp.where(first_half, s1, s0)
+    q_own = valence_values.reshape(128, 256)
+    par1 = swap(jnp.concatenate([q_own, give], axis=0))
+
     cond_row = jnp.pad(conduction_energy.reshape(1, 32), ((0, 7), (0, 224)))
-    q_own = valence_values.reshape(128, 256)
-    p_own = conduction_values.reshape(128, 256)
-    par1 = swap(jnp.concatenate([q_own, give, cond_row], axis=0))
     w_own = jnp.concatenate(
         [screened[part, 32 * at : 32 * at + 32] for at in range(2) for part in range(2)], axis=-1
     ).reshape(256, 256)
-    par2 = swap(jnp.concatenate([p_own, w_own], axis=0))
+    own2 = jnp.concatenate([conduction_values.reshape(128, 256), w_own, cond_row], axis=0)
+    par2 = swap(own2)
 
     own4 = gather_x(jnp.concatenate([q_own, keep], axis=0))
-    par4 = gather_x(par1[:192])
+    par4 = gather_x(par1)
 
     def ordered(own, par, axis):
         return jnp.where(
             first_half, jnp.stack([own, par], axis=axis), jnp.stack([par, own], axis=axis)
         )
 
-    own_cond = conduction_energy[:, 0]
-    par_cond = par1[192, :32]
-    energy = (ordered(own_cond, par_cond, 0)[:, :, None] - valence_energy[0][None, None])[:, None]
-    own_energy = own_cond[:, None] - valence_energy[0][None]
-    state_q = ordered(keep.reshape(2, 32, 256), par1[128:192].reshape(2, 32, 256), 0)
-
-    weight = transform_weights(zh_scalar, w_own, par2)
+    weight = transform_weights(zh_scalar, own2, par2)
+    cond = ordered(own2[384, :32], par2[384, :32], 0)
+    energy = cond[:, :, None] - valence_energy[0][None, None]
+    own_energy = own2[384, :32][:, None] - valence_energy[0][None]
+    state_q = ordered(keep.reshape(2, 32, 256), par1[128:].reshape(2, 32, 256), 0)
     own4, par4, weight, place, energy, own_energy, state_q = lax.optimization_barrier(
         (own4, par4, weight, place, energy, own_energy, state_q)
     )
-    pc_h, pc_l, qc_h, qc_l, pairs = first(zh_scalar, own4, par4, p_own, par2)
+    pc_h, pc_l, qc_h, qc_l, pairs = first(zh_scalar, own4, par4, own2, par2)
     pc, qc = (pc_h, pc_l), (qc_h, qc_l)
 
     def convolve(block):
@@ -343,18 +356,13 @@
         return backward(back, pc, qc)
 
     parts = exchange(convolve(pairs).reshape(4, 128, 256), "x")
-    parts = parts.reshape(4, 2, 2, 32, 256)
-    state_q = energy * state_q + jnp.sum(parts, axis=0)
-    state_all = gather_x(state_q)
-
-    keep = jnp.where(first_half, state_q[0], state_q[1])
-    give = jnp.where(first_half, state_q[1], state_q[0])
-    got = swap(give.reshape(64, 256)).reshape(2, 32, 256)
-    once = place_once(zh_scalar, keep, got)
+    state_four, keep, give = update(zh_scalar, state_q, energy, parts)
+    got = swap(give)
+    state_all = exchange(state_four, "x")
 
     pairs = forward(state_all, pc, qc)
     parts = exchange(convolve(pairs).reshape(8, 64, 256), ROWS)
-    return once, place_twice(once, own_energy, parts)
+    return finish(zh_scalar, keep, got, own_energy, parts)
 
 
 def solution(mesh):

time: 204 us -> 207 us (1.015)
  the two profiles are of different devices: /device:TPU:8 before, /device:TPU:72 now
where the time goes in v2:
time: 207 us; the launch traced here: 206 us
  blocking collectives  125 us (60%)
  starting transfers between devices  37.7 us (18%)
  waiting for transfers between devices  29.3 us (14%)
  Pallas kernels  8.47 us (4%)
  local copies, waits for them, and re-layouts  4.42 us (2%)
    all_to_all x6, blocking collectives, exchange(): return lax.all_to_all(value, axes, split_axis=0, concat_axis=0, tiled=True)  125 us
    ppermute x3, waiting for transfers between devices, swap(): return lax.ppermute(value, 'zh', [(0, 1), (1, 0)])  23.1 us
    ppermute x3, starting transfers between devices, swap(): return lax.ppermute(value, 'zh', [(0, 1), (1, 0)])  19.8 us
    all_to_all x3, starting transfers between devices, exchange(): return lax.all_to_all(value, axes, split_axis=0, concat_axis=0, tiled=True)  17.9 us
    all_to_all x3, waiting for transfers between devices, exchange(): return lax.all_to_all(value, axes, split_axis=0, concat_axis=0, tiled=True)  6.17 us
  transfers between devices with their start and end apart: 6, of which 5 were waited for; matrix products, arithmetic and copies ran while one was open for 1% of the time, Pallas kernels for 0%

profile of v2, /device:TPU:72, one launch (start us, length us, event | category | flops | bytes accessed | tf_op | source)
XLA Modules:
  0.0 206.3 jit_solution(12299125375369433638)
XLA Ops:
  0.6 1.0 copy.15
  1.7 1.0 broadcast_in_dim.19
  2.7 4.4 %all-to-all-start = ((f32[4,192,256]{2,1,0:T(8,128)}), f32[4,192,256]{2,1,0:T(8,128)S(1)}, u32[]{:S(2)}, u32[]{:S(2)}) async-start(f32[4,192,256]{2,1,0:T(8,128)} %broadcast_in_dim.19), calls=%async_computation | async-start | bytes 1572864 | tf_op jit(solution)/shard_map/all_to_all | solution.py:291
  7.1 10.0 %collective-permute-start = (f32[192,256]{1,0:T(8,128)S(1)}, f32[192,256]{1,0:T(8,128)S(1)}, u32[]{:S(2)}, u32[]{:S(2)}) collective-permute-start(f32[192,256]{1,0:T(8,128)S(1)} %get-tuple-element.36), channel_id=1, source_target_pairs={{0,1},{1,0},{2,3},{3,2},{4,5},{5,4},{6,7},{7,6},{8,9},{9,8},{10,11... | collective-permute-start | bytes 589832 | tf_op jit(solution)/shard_map/ppermute | solution.py:299
  17.2 0.6 copy-done.4
  17.9 0.2 select_maximum_fusion.own.p_own
  18.0 1.9 collective-permute-start.1
  20.0 0.7 copy-done.5
  20.7 5.8 %collective-permute-done = f32[192,256]{1,0:T(8,128)S(1)} collective-permute-done((f32[192,256]{1,0:T(8,128)S(1)}, f32[192,256]{1,0:T(8,128)S(1)}, u32[]{:S(2)}, u32[]{:S(2)}) %collective-permute-start) | collective-permute-done | bytes 196640 | tf_op jit(solution)/shard_map/ppermute | solution.py:299
  26.5 1.0 broadcast_in_dim.32
  27.5 4.9 %all-to-all-start.1 = ((f32[4,192,256]{2,1,0:T(8,128)}), f32[4,192,256]{2,1,0:T(8,128)S(1)}, u32[]{:S(2)}, u32[]{:S(2)}) async-start(f32[4,192,256]{2,1,0:T(8,128)} %broadcast_in_dim.32), calls=%async_computation.1 | async-start | bytes 1572864 | tf_op jit(solution)/shard_map/all_to_all | solution.py:291
  32.6 0.1 select_reduce_fusion.place
  32.7 4.2 %collective-permute-done.1.par.p_par = f32[392,256]{1,0:T(8,128)S(1)} collective-permute-done((f32[392,256]{1,0:T(8,128)S(1)}, f32[392,256]{1,0:T(8,128)S(1)}, u32[]{:S(2)}, u32[]{:S(2)}) %collective-permute-start.1) | collective-permute-done | bytes 401440 | tf_op jit(solution)/shard_map/ppermute | solution.py:299
  36.9 0.3 weights.1.weight
  37.3 4.6 %all-to-all-done.1.par = f32[4,192,256]{2,1,0:T(8,128)S(1)} async-done(((f32[4,192,256]{2,1,0:T(8,128)}), f32[4,192,256]{2,1,0:T(8,128)S(1)}, u32[]{:S(2)}, u32[]{:S(2)}) %all-to-all-start.1) | async-done | bytes 786464 | tf_op jit(solution)/shard_map/all_to_all | solution.py:291
  41.9 1.1 first.1
  43.0 30.4 %all_to_all.45.block = f32[64,16,128]{2,1,0:T(8,128)S(1)} all-to-all(f32[64,16,128]{2,1,0:T(8,128)S(1)} %get-tuple-element.22), channel_id=1, replica_groups=mesh['zl'=4,'y'=8,'core'=2,'x'=4,'zh'=2] {'zl','y','core'}, dimensions={0} | all-to-all | bytes 1048576 | tf_op jit(solution)/shard_map/all_to_all | solution.py:291
  73.5 0.9 spectral.2
  74.3 23.1 %all_to_all.46.block = f32[64,16,128]{2,1,0:T(8,128)S(1)} all-to-all(f32[64,16,128]{2,1,0:T(8,128)S(1)} %spectral.2), channel_id=1, replica_groups=mesh['zl'=4,'y'=8,'core'=2,'x'=4,'zh'=2] {'zl','y','core'}, dimensions={0} | all-to-all | bytes 1048576 | tf_op jit(solution)/shard_map/all_to_all | solution.py:291
  97.4 1.3 backward.2
  98.7 14.6 %all_to_all.47.parts = f32[4,128,256]{2,1,0:T(8,128)S(1)} all-to-all(f32[4,128,256]{2,1,0:T(8,128)S(1)} %bitcast.32), channel_id=1, replica_groups=mesh['zl'=4,'y'=8,'core'=2,'x'=4,'zh'=2] {'x'}, dimensions={0} | all-to-all | bytes 1048576 | tf_op jit(solution)/shard_map/all_to_all | solution.py:291
  113.4 11.7 %all_to_all.48.state = f32[4,2,2,32,256]{4,3,2,1,0:T(8,128)S(1)} all-to-all(f32[4,2,2,32,256]{4,3,2,1,0:T(8,128)S(1)} %get-tuple-element.31), channel_id=1, replica_groups=mesh['zl'=4,'y'=8,'core'=2,'x'=4,'zh'=2] {'x'}, dimensions={0} | all-to-all | bytes 1048576 | tf_op jit(solution)/shard_map/all_to_all | solution.py:291
  125.0 1.0 forward.1
  126.0 22.4 %all_to_all.49.block = f32[64,16,128]{2,1,0:T(8,128)S(1)} all-to-all(f32[64,16,128]{2,1,0:T(8,128)S(1)} %forward.1), channel_id=1, replica_groups=mesh['zl'=4,'y'=8,'core'=2,'x'=4,'zh'=2] {'zl','y','core'}, dimensions={0} | all-to-all | bytes 1048576 | tf_op jit(solution)/shard_map/all_to_all | solution.py:291
  148.4 0.9 spectral.3
  149.3 23.1 %all_to_all.50.block = f32[64,16,128]{2,1,0:T(8,128)S(1)} all-to-all(f32[64,16,128]{2,1,0:T(8,128)S(1)} %spectral.3), channel_id=1, replica_groups=mesh['zl'=4,'y'=8,'core'=2,'x'=4,'zh'=2] {'zl','y','core'}, dimensions={0} | all-to-all | bytes 1048576 | tf_op jit(solution)/shard_map/all_to_all | solution.py:291
  172.3 2.1 %backward.3 = f32[8,2,32,256]{3,2,1,0:T(8,128)} custom-call(f32[64,16,128]{2,1,0:T(8,128)S(1)} %all_to_all.50.block, bf16[128,512]{1,0:T(8,128)(2,1)S(1)} %get-tuple-element.24.pc_h, bf16[128,512]{1,0:T(8,128)(2,1)S(1)} %get-tuple-element.25.pc_l, bf16[512,512]{1,0:T(8,128)(2,1)S(1)} %get-tuple-element.26.qc_h, bf16[512,512]{1,0:T(8,128)(2,1)S(1)} %get-tuple-element.27.qc_l), custom_call_target="tpu_custom_call" | custom-call | tf_op jit(solution)/shard_map/backward/pallas_call | solution.py:134
  174.4 8.5 %all-to-all-start.8 = ((f32[8,64,256]{2,1,0:T(8,128)}), f32[8,64,256]{2,1,0:T(8,128)S(1)}, u32[]{:S(2)}, u32[]{:S(2)}) async-start(f32[8,64,256]{2,1,0:T(8,128)} %bitcast.20), calls=%async_computation.8 | async-start | bytes 1048576 | tf_op jit(solution)/shard_map/all_to_all | solution.py:291
  183.0 7.8 %collective-permute-start.2 = (f32[64,256]{1,0:T(8,128)S(1)}, f32[64,256]{1,0:T(8,128)S(1)}, u32[]{:S(2)}, u32[]{:S(2)}) collective-permute-start(f32[64,256]{1,0:T(8,128)S(1)} %get-tuple-element.29), channel_id=1, source_target_pairs={{0,1},{1,0},{2,3},{3,2},{4,5},{5,4},{6,7},{7,6},{8,9},{9,8},{10,11... | collective-permute-start | bytes 196616 | tf_op jit(solution)/shard_map/ppermute | solution.py:299
  190.8 13.0 %collective-permute-done.2.got = f32[64,256]{1,0:T(8,128)S(1)} collective-permute-done((f32[64,256]{1,0:T(8,128)S(1)}, f32[64,256]{1,0:T(8,128)S(1)}, u32[]{:S(2)}, u32[]{:S(2)}) %collective-permute-start.2) | collective-permute-done | bytes 65568 | tf_op jit(solution)/shard_map/ppermute | solution.py:299
  203.9 1.5 all-to-all-done.8.parts
  205.4 0.9 finish.1
  (24 shorter events, 0.5 us)
Async XLA Ops:
  0.6 1.0 copy-start.1
  2.7 14.4 %copy-start.2 = (f32[2,64,1,256]{3,2,1,0:T(1,128)S(1)}, f32[2,64,1,256]{3,2,1,0:T(1,128)}, u32[]{:S(2)}) copy-start(f32[2,64,1,256]{3,2,1,0:T(1,128)} %param.8) | copy-start | bytes 393220
  2.7 14.5 %copy-start = (f32[2,64,8,64]{3,2,1,0:T(8,128)S(1)}, f32[2,64,8,64]{3,2,1,0:T(8,128)}, u32[]{:S(2)}) copy-start(f32[2,64,8,64]{3,2,1,0:T(8,128)} %param.10) | copy-start | bytes 786436
  2.7 23.9 %all-to-all-start = ((f32[4,192,256]{2,1,0:T(8,128)}), f32[4,192,256]{2,1,0:T(8,128)S(1)}, u32[]{:S(2)}, u32[]{:S(2)}) async-start(f32[4,192,256]{2,1,0:T(8,128)} %broadcast_in_dim.19), calls=%async_computation | async-start | bytes 1572864 | tf_op jit(solution)/shard_map/all_to_all | solution.py:291
  7.1 19.4 %collective-permute-start = (f32[192,256]{1,0:T(8,128)S(1)}, f32[192,256]{1,0:T(8,128)S(1)}, u32[]{:S(2)}, u32[]{:S(2)}) collective-permute-start(f32[192,256]{1,0:T(8,128)S(1)} %get-tuple-element.36), channel_id=1, source_target_pairs={{0,1},{1,0},{2,3},{3,2},{4,5},{5,4},{6,7},{7,6},{8,9},{9,8},{10,11... | collective-permute-start | bytes 589832 | tf_op jit(solution)/shard_map/ppermute | solution.py:299
  17.2 0.7 copy-start.4
  18.0 18.9 %collective-permute-start.1 = (f32[392,256]{1,0:T(8,128)S(1)}, f32[392,256]{1,0:T(8,128)S(1)}, u32[]{:S(2)}, u32[]{:S(2)}) collective-permute-start(f32[392,256]{1,0:T(8,128)S(1)} %select_maximum_fusion.own.p_own), channel_id=1, source_target_pairs={{0,1},{1,0},{2,3},{3,2},{4,5},{5,4},{6,7},{7,6},{8,9},{9,8},{10,11... | collective-permute-start | bytes 1204232 | tf_op jit(solution)/shard_map/ppermute | solution.py:299
  20.0 0.7 copy-start.5
  27.5 4.9 %copy-start.3 = (s32[64,64]{1,0:T(8,128)S(1)}, s32[64,64]{1,0:T(8,128)}, u32[]{:S(2)}) copy-start(s32[64,64]{1,0:T(8,128)} %param.13) | copy-start | bytes 49156
  27.5 14.4 %all-to-all-start.1 = ((f32[4,192,256]{2,1,0:T(8,128)}), f32[4,192,256]{2,1,0:T(8,128)S(1)}, u32[]{:S(2)}, u32[]{:S(2)}) async-start(f32[4,192,256]{2,1,0:T(8,128)} %broadcast_in_dim.32), calls=%async_computation.1 | async-start | bytes 1572864 | tf_op jit(solution)/shard_map/all_to_all | solution.py:291
  174.4 31.0 %all-to-all-start.8 = ((f32[8,64,256]{2,1,0:T(8,128)}), f32[8,64,256]{2,1,0:T(8,128)S(1)}, u32[]{:S(2)}, u32[]{:S(2)}) async-start(f32[8,64,256]{2,1,0:T(8,128)} %bitcast.20), calls=%async_computation.8 | async-start | bytes 1048576 | tf_op jit(solution)/shard_map/all_to_all | solution.py:291
  183.0 20.9 %collective-permute-start.2 = (f32[64,256]{1,0:T(8,128)S(1)}, f32[64,256]{1,0:T(8,128)S(1)}, u32[]{:S(2)}, u32[]{:S(2)}) collective-permute-start(f32[64,256]{1,0:T(8,128)S(1)} %get-tuple-element.29), channel_id=1, source_target_pairs={{0,1},{1,0},{2,3},{3,2},{4,5},{5,4},{6,7},{7,6},{8,9},{9,8},{10,11... | collective-permute-start | bytes 196616 | tf_op jit(solution)/shard_map/ppermute | solution.py:299

commit v3 on v2

--- a/solution.py
+++ b/solution.py
@@ -58,7 +58,7 @@
     out[:, 8:16, :] = pairs[:, 128:].reshape(64, 8, 128)
 
 
-def first_kernel(zh, own, par, p_own, p_par, pc_h, pc_l, qc_h, qc_l, out):
+def first_kernel(zh, own, par, pc_h, pc_l, qc_h, qc_l, out):
     mine = zh[0]
     real, imag = [], []
     for x in range(4):
@@ -73,32 +73,23 @@
                 source = pl.ds(128 + part * 32, 32)
                 piece = jnp.where(mine == h, own[x, source, :], par[x, source, :])
                 (imag if part else real).append(piece)
-    for h in range(2):
-        for part in range(2):
-            source = pl.ds(part * 64, 64)
-            piece = jnp.where(mine == h, p_own[source, :], p_par[source, :])
-            high, low = split(piece)
-            pc_h[pl.ds(h * 64, 64), pl.ds(part * 256, 256)] = high
-            pc_l[pl.ds(h * 64, 64), pl.ds(part * 256, 256)] = low
     real, imag = jnp.concatenate(real, axis=0), jnp.concatenate(imag, axis=0)
     multiply_out(real, imag, pc_h, pc_l, qc_h, qc_l, out)
 
 
-def first(zh, own, par, p_own, p_par):
+def first(zh, own, par, pc):
     return pl.pallas_call(
         first_kernel,
         out_shape=(
-            shape((128, 512), BF16),
-            shape((128, 512), BF16),
             shape((512, 512), BF16),
             shape((512, 512), BF16),
             shape((64, 16, 128)),
         ),
         in_specs=[SMEM] + [VMEM] * 4,
-        out_specs=(VMEM,) * 5,
+        out_specs=(VMEM,) * 3,
         name="first",
         compiler_params=PARAMS,
-    )(zh, own, par, p_own, p_par)
+    )(zh, own, par, *pc)
 
 
 def forward_kernel(state, pc_h, pc_l, qc_h, qc_l, out):
@@ -118,13 +109,17 @@
     )(state, *pc, *qc)
 
 
-def backward_kernel(block, pc_h, pc_l, qc_h, qc_l, out):
+def second_term(block, pc_h, pc_l, qc_h, qc_l):
     real = block[:, 0:8, :].reshape(512, 128)
     imag = block[:, 8:16, :].reshape(512, 128)
     valence = (transposed(qc_h), transposed(qc_l))
     mixed = dot3(valence, split(complex_pair(real, imag)), NN)
     conduction = (transposed(pc_h), transposed(pc_l))
-    term = dot3(conduction, with_turned(mixed), NT)
+    return dot3(conduction, with_turned(mixed), NT)
+
+
+def backward_kernel(block, pc_h, pc_l, qc_h, qc_l, out):
+    term = second_term(block, pc_h, pc_l, qc_h, qc_l)
     for row in range(8):
         out[row, 0] = term[row * 32 : row * 32 + 32, :256]
         out[row, 1] = term[row * 32 : row * 32 + 32, 256:]
@@ -139,6 +134,29 @@
         name="backward",
         compiler_params=PARAMS,
     )(block, *pc, *qc)
+
+
+def backward_apart_kernel(zh, block, pc_h, pc_l, qc_h, qc_l, mine_out, other_out):
+    mine = zh[0]
+    term = second_term(block, pc_h, pc_l, qc_h, qc_l)
+    for x in range(4):
+        for part in range(2):
+            columns = slice(256 * part, 256 * part + 256)
+            low = term[64 * x : 64 * x + 32, columns]
+            high = term[64 * x + 32 : 64 * x + 64, columns]
+            mine_out[x, pl.ds(32 * part, 32), :] = jnp.where(mine == 0, low, high)
+            other_out[x, pl.ds(32 * part, 32), :] = jnp.where(mine == 0, high, low)
+
+
+def backward_apart(zh, block, pc, qc):
+    return pl.pallas_call(
+        backward_apart_kernel,
+        out_shape=(shape((4, 64, 256)),) * 2,
+        in_specs=[SMEM] + [VMEM] * 5,
+        out_specs=(VMEM,) * 2,
+        name="backward_apart",
+        compiler_params=PARAMS,
+    )(zh, block, *pc, *qc)
 
 
 def update_kernel(zh, state, energy, parts, out, keep, give):
@@ -168,32 +186,52 @@
     )(zh, state, energy, parts)
 
 
-def finish_kernel(zh, keep, got, energy, parts, once, twice):
+def total(parts, rows):
+    return (parts[0, rows, :] + parts[1, rows, :]) + (parts[2, rows, :] + parts[3, rows, :])
+
+
+def other_half_kernel(zh, energy, give, parts, out):
+    factor = jnp.where(zh[0] == 0, energy[1], energy[0])
+    for part in range(2):
+        rows = pl.ds(32 * part, 32)
+        out[rows, :] = factor * give[rows, :] + total(parts, rows)
+
+
+def other_half(zh, energy, give, parts):
+    return pl.pallas_call(
+        other_half_kernel,
+        out_shape=shape((64, 256)),
+        in_specs=[SMEM] + [VMEM] * 3,
+        out_specs=VMEM,
+        name="other_half",
+        compiler_params=PARAMS,
+    )(zh, energy, give, parts)
+
+
+def finish_kernel(zh, keep, got, energy, parts, got_twice, once, twice):
     mine = zh[0]
-    factor = energy[...]
-    factor = jnp.stack([factor, factor], axis=1)
+    factor = jnp.where(mine == 0, energy[0], energy[1])
+
+    def both(here, there):
+        low, high = jnp.where(mine == 0, here, there), jnp.where(mine == 0, there, here)
+        return jnp.stack([low, high], axis=1)
+
     for part in range(2):
-        here, there = keep[part], got[pl.ds(32 * part, 32), :]
-        low = jnp.where(mine == 0, here, there)
-        high = jnp.where(mine == 0, there, here)
-        before = jnp.stack([low, high], axis=1)
-        terms = []
-        for vector in range(2):
-            rows = [parts[2 * x + vector, pl.ds(32 * part, 32), :] for x in range(4)]
-            terms.append((rows[0] + rows[1]) + (rows[2] + rows[3]))
-        once[:, 0, part] = before
-        twice[:, 0, part] = factor * before + jnp.stack(terms, axis=1)
-
-
-def finish(zh, keep, got, energy, parts):
+        rows = pl.ds(32 * part, 32)
+        once[:, 0, part] = both(keep[part], got[rows, :])
+        own = factor * keep[part] + total(parts, rows)
+        twice[:, 0, part] = both(own, got_twice[rows, :])
+
+
+def finish(zh, keep, got, energy, parts, got_twice):
     return pl.pallas_call(
         finish_kernel,
         out_shape=(shape((32, 1, 2, 2, 256)),) * 2,
-        in_specs=[SMEM] + [VMEM] * 4,
+        in_specs=[SMEM] + [VMEM] * 5,
         out_specs=(VMEM,) * 2,
         name="finish",
         compiler_params=PARAMS,
-    )(zh, keep, got, energy, parts)
+    )(zh, keep, got, energy, parts, got_twice)
 
 
 def butterfly(values, sign):
@@ -221,8 +259,15 @@
     ref[index, 0:8, :], ref[index, 8:16, :] = value
 
 
-def weights_kernel(zh, own, par, out):
+def weights_kernel(zh, own, par, out, pc_h, pc_l):
     mine = zh[0]
+    for h in range(2):
+        for part in range(2):
+            source = pl.ds(part * 64, 64)
+            piece = jnp.where(mine == h, own[source, :], par[source, :])
+            high, low = split(piece)
+            pc_h[pl.ds(h * 64, 64), pl.ds(part * 256, 256)] = high
+            pc_l[pl.ds(h * 64, 64), pl.ds(part * 256, 256)] = low
     lane = lax.broadcasted_iota(jnp.int32, (8, 128), 1)
     for a in range(4):
         values = []
@@ -247,9 +292,9 @@
 def transform_weights(zh, own, par):
     return pl.pallas_call(
         weights_kernel,
-        out_shape=shape((64, 16, 128)),
+        out_shape=(shape((64, 16, 128)), shape((128, 512), BF16), shape((128, 512), BF16)),
         in_specs=[SMEM, VMEM, VMEM],
-        out_specs=VMEM,
+        out_specs=(VMEM,) * 3,
         name="weights",
         compiler_params=PARAMS,
     )(zh, own, par)
@@ -339,30 +384,33 @@
             first_half, jnp.stack([own, par], axis=axis), jnp.stack([par, own], axis=axis)
         )
 
-    weight = transform_weights(zh_scalar, own2, par2)
+    weight, pc_h, pc_l = transform_weights(zh_scalar, own2, par2)
     cond = ordered(own2[384, :32], par2[384, :32], 0)
     energy = cond[:, :, None] - valence_energy[0][None, None]
-    own_energy = own2[384, :32][:, None] - valence_energy[0][None]
     state_q = ordered(keep.reshape(2, 32, 256), par1[128:].reshape(2, 32, 256), 0)
-    own4, par4, weight, place, energy, own_energy, state_q = lax.optimization_barrier(
-        (own4, par4, weight, place, energy, own_energy, state_q)
+    own4, par4, weight, pc_h, pc_l, place, energy, state_q = lax.optimization_barrier(
+        (own4, par4, weight, pc_h, pc_l, place, energy, state_q)
     )
-    pc_h, pc_l, qc_h, qc_l, pairs = first(zh_scalar, own4, par4, own2, par2)
-    pc, qc = (pc_h, pc_l), (qc_h, qc_l)
+    pc = (pc_h, pc_l)
+    qc_h, qc_l, pairs = first(zh_scalar, own4, par4, pc)
+    qc = (qc_h, qc_l)
 
     def convolve(block):
         sent = exchange(block, KA)
-        back = exchange(spectral(place, sent, weight), KA)
-        return backward(back, pc, qc)
-
-    parts = exchange(convolve(pairs).reshape(4, 128, 256), "x")
+        return exchange(spectral(place, sent, weight), KA)
+
+    term = backward(convolve(pairs), pc, qc)
+    parts = exchange(term.reshape(4, 128, 256), "x")
     state_four, keep, give = update(zh_scalar, state_q, energy, parts)
     got = swap(give)
     state_all = exchange(state_four, "x")
 
-    pairs = forward(state_all, pc, qc)
-    parts = exchange(convolve(pairs).reshape(8, 64, 256), ROWS)
-    return finish(zh_scalar, keep, got, own_energy, parts)
+    back = convolve(forward(state_all, pc, qc))
+    mine, other = backward_apart(zh_scalar, back, pc, qc)
+    other = exchange(other, "x")
+    got_twice = swap(other_half(zh_scalar, energy, give, other))
+    mine = exchange(mine, "x")
+    return finish(zh_scalar, keep, got, energy, mine, got_twice)
 
 
 def solution(mesh):

time: 207 us -> 212 us (1.024)
  the two profiles are of different devices: /device:TPU:72 before, /device:TPU:2 now
where the time goes in v3:
time: 212 us; the launch traced here: 211 us
  blocking collectives  130 us (61%)
  starting transfers between devices  38.8 us (18%)
  waiting for transfers between devices  28 us (13%)
  Pallas kernels  8.34 us (4%)
  local copies, waits for them, and re-layouts  4.39 us (2%)
    all_to_all x7, blocking collectives, exchange(): return lax.all_to_all(value, axes, split_axis=0, concat_axis=0, tiled=True)  130 us
    ppermute x4, waiting for transfers between devices, swap(): return lax.ppermute(value, 'zh', [(0, 1), (1, 0)])  28 us
    ppermute x4, starting transfers between devices, swap(): return lax.ppermute(value, 'zh', [(0, 1), (1, 0)])  19.6 us
    all_to_all x3, starting transfers between devices, exchange(): return lax.all_to_all(value, axes, split_axis=0, concat_axis=0, tiled=True)  19.2 us
  transfers between devices with their start and end apart: 7, of which 4 were waited for; matrix products, arithmetic and copies ran while one was open for 1% of the time, Pallas kernels for 0%

profile of v3, /device:TPU:2, one launch (start us, length us, event | category | flops | bytes accessed | tf_op | source)
XLA Modules:
  0.0 211.1 jit_solution(2512662781852088787)
XLA Ops:
  0.6 1.0 copy.15
  1.7 1.0 broadcast_in_dim.19
  2.7 9.5 %all-to-all-start = ((f32[4,192,256]{2,1,0:T(8,128)}), f32[4,192,256]{2,1,0:T(8,128)S(1)}, u32[]{:S(2)}, u32[]{:S(2)}) async-start(f32[4,192,256]{2,1,0:T(8,128)} %broadcast_in_dim.19), calls=%async_computation | async-start | bytes 1572864 | tf_op jit(solution)/shard_map/all_to_all | solution.py:336
  12.1 6.5 %collective-permute-start = (f32[192,256]{1,0:T(8,128)S(1)}, f32[192,256]{1,0:T(8,128)S(1)}, u32[]{:S(2)}, u32[]{:S(2)}) collective-permute-start(f32[192,256]{1,0:T(8,128)S(1)} %get-tuple-element.44), channel_id=1, source_target_pairs={{0,1},{1,0},{2,3},{3,2},{4,5},{5,4},{6,7},{7,6},{8,9},{9,8},{10,11... | collective-permute-start | bytes 589832 | tf_op jit(solution)/shard_map/ppermute | solution.py:344
  18.8 0.6 copy-done.4
  19.4 0.2 select_maximum_fusion.own
  19.6 3.3 %collective-permute-start.1 = (f32[392,256]{1,0:T(8,128)S(1)}, f32[392,256]{1,0:T(8,128)S(1)}, u32[]{:S(2)}, u32[]{:S(2)}) collective-permute-start(f32[392,256]{1,0:T(8,128)S(1)} %select_maximum_fusion.own), channel_id=1, source_target_pairs={{0,1},{1,0},{2,3},{3,2},{4,5},{5,4},{6,7},{7,6},{8,9},{9,8},{10,11... | collective-permute-start | bytes 1204232 | tf_op jit(solution)/shard_map/ppermute | solution.py:344
  22.9 5.0 %collective-permute-done = f32[192,256]{1,0:T(8,128)S(1)} collective-permute-done((f32[192,256]{1,0:T(8,128)S(1)}, f32[192,256]{1,0:T(8,128)S(1)}, u32[]{:S(2)}, u32[]{:S(2)}) %collective-permute-start) | collective-permute-done | bytes 196640 | tf_op jit(solution)/shard_map/ppermute | solution.py:344
  27.9 1.0 broadcast_in_dim.32
  28.9 4.9 %all-to-all-start.1 = ((f32[4,192,256]{2,1,0:T(8,128)}), f32[4,192,256]{2,1,0:T(8,128)S(1)}, u32[]{:S(2)}, u32[]{:S(2)}) async-start(f32[4,192,256]{2,1,0:T(8,128)} %broadcast_in_dim.32), calls=%async_computation.1 | async-start | bytes 1572864 | tf_op jit(solution)/shard_map/all_to_all | solution.py:336
  34.1 13.5 %collective-permute-done.1.par = f32[392,256]{1,0:T(8,128)S(1)} collective-permute-done((f32[392,256]{1,0:T(8,128)S(1)}, f32[392,256]{1,0:T(8,128)S(1)}, u32[]{:S(2)}, u32[]{:S(2)}) %collective-permute-start.1) | collective-permute-done | bytes 401440 | tf_op jit(solution)/shard_map/ppermute | solution.py:344
  47.6 0.3 weights.1
  47.9 0.7 copy-done.5
  48.7 1.0 first.1
  49.7 27.2 %all_to_all.50.block = f32[64,16,128]{2,1,0:T(8,128)S(1)} all-to-all(f32[64,16,128]{2,1,0:T(8,128)S(1)} %get-tuple-element.31), channel_id=1, replica_groups=mesh['zl'=4,'y'=8,'core'=2,'x'=4,'zh'=2] {'zl','y','core'}, dimensions={0} | all-to-all | bytes 1048576 | tf_op jit(solution)/shard_map/all_to_all | solution.py:336
  76.9 0.9 spectral.2
  77.8 23.1 %all_to_all.51.block = f32[64,16,128]{2,1,0:T(8,128)S(1)} all-to-all(f32[64,16,128]{2,1,0:T(8,128)S(1)} %spectral.2), channel_id=1, replica_groups=mesh['zl'=4,'y'=8,'core'=2,'x'=4,'zh'=2] {'zl','y','core'}, dimensions={0} | all-to-all | bytes 1048576 | tf_op jit(solution)/shard_map/all_to_all | solution.py:336
  100.8 1.3 backward.1
  102.2 12.8 %all_to_all.52.parts = f32[4,128,256]{2,1,0:T(8,128)S(1)} all-to-all(f32[4,128,256]{2,1,0:T(8,128)S(1)} %bitcast.30), channel_id=1, replica_groups=mesh['zl'=4,'y'=8,'core'=2,'x'=4,'zh'=2] {'x'}, dimensions={0} | all-to-all | bytes 1048576 | tf_op jit(solution)/shard_map/all_to_all | solution.py:336
  115.0 10.9 %all_to_all.53.state = f32[4,2,2,32,256]{4,3,2,1,0:T(8,128)S(1)} all-to-all(f32[4,2,2,32,256]{4,3,2,1,0:T(8,128)S(1)} %get-tuple-element.37), channel_id=1, replica_groups=mesh['zl'=4,'y'=8,'core'=2,'x'=4,'zh'=2] {'x'}, dimensions={0} | all-to-all | bytes 1048576 | tf_op jit(solution)/shard_map/all_to_all | solution.py:336
  125.9 1.0 forward.1
  126.9 23.7 %all_to_all.54.block = f32[64,16,128]{2,1,0:T(8,128)S(1)} all-to-all(f32[64,16,128]{2,1,0:T(8,128)S(1)} %forward.1), channel_id=1, replica_groups=mesh['zl'=4,'y'=8,'core'=2,'x'=4,'zh'=2] {'zl','y','core'}, dimensions={0} | all-to-all | bytes 1048576 | tf_op jit(solution)/shard_map/all_to_all | solution.py:336
  150.6 0.9 spectral.3
  151.5 23.1 %all_to_all.55.block = f32[64,16,128]{2,1,0:T(8,128)S(1)} all-to-all(f32[64,16,128]{2,1,0:T(8,128)S(1)} %spectral.3), channel_id=1, replica_groups=mesh['zl'=4,'y'=8,'core'=2,'x'=4,'zh'=2] {'zl','y','core'}, dimensions={0} | all-to-all | bytes 1048576 | tf_op jit(solution)/shard_map/all_to_all | solution.py:336
  174.6 2.0 backward_apart.1
  176.6 9.5 %all_to_all.56.parts = f32[4,64,256]{2,1,0:T(8,128)S(1)} all-to-all(f32[4,64,256]{2,1,0:T(8,128)S(1)} %get-tuple-element.39), channel_id=1, replica_groups=mesh['zl'=4,'y'=8,'core'=2,'x'=4,'zh'=2] {'x'}, dimensions={0} | all-to-all | bytes 524288 | tf_op jit(solution)/shard_map/all_to_all | solution.py:336
  186.1 4.8 %all-to-all-start.8 = ((f32[4,64,256]{2,1,0:T(8,128)}), f32[4,64,256]{2,1,0:T(8,128)S(1)}, u32[]{:S(2)}, u32[]{:S(2)}) async-start(f32[4,64,256]{2,1,0:T(8,128)} %get-tuple-element.38), calls=%async_computation.8 | async-start | bytes 524288 | tf_op jit(solution)/shard_map/all_to_all | solution.py:336
  190.9 7.8 %collective-permute-start.2 = (f32[64,256]{1,0:T(8,128)S(1)}, f32[64,256]{1,0:T(8,128)S(1)}, u32[]{:S(2)}, u32[]{:S(2)}) collective-permute-start(f32[64,256]{1,0:T(8,128)S(1)} %get-tuple-element.36.give), channel_id=1, source_target_pairs={{0,1},{1,0},{2,3},{3,2},{4,5},{5,4},{6,7},{7,6},{8,9},{9,8},{10,11... | collective-permute-start | bytes 196616 | tf_op jit(solution)/shard_map/ppermute | solution.py:344
  198.8 1.9 collective-permute-start.3
  200.7 0.8 collective-permute-done.2.got
  201.5 8.7 %collective-permute-done.3.got_twice = f32[64,256]{1,0:T(8,128)S(1)} collective-permute-done((f32[64,256]{1,0:T(8,128)S(1)}, f32[64,256]{1,0:T(8,128)S(1)}, u32[]{:S(2)}, u32[]{:S(2)}) %collective-permute-start.3) | collective-permute-done | bytes 65568 | tf_op jit(solution)/shard_map/ppermute | solution.py:344
  210.2 0.9 finish.1
  (27 shorter events, 0.5 us)
Async XLA Ops:
  0.6 1.0 copy-start.1
  2.7 16.0 %copy-start = (f32[2,64,8,64]{3,2,1,0:T(8,128)S(1)}, f32[2,64,8,64]{3,2,1,0:T(8,128)}, u32[]{:S(2)}) copy-start(f32[2,64,8,64]{3,2,1,0:T(8,128)} %param.10) | copy-start | bytes 786436
  2.7 25.3 %all-to-all-start = ((f32[4,192,256]{2,1,0:T(8,128)}), f32[4,192,256]{2,1,0:T(8,128)S(1)}, u32[]{:S(2)}, u32[]{:S(2)}) async-start(f32[4,192,256]{2,1,0:T(8,128)} %broadcast_in_dim.19), calls=%async_computation | async-start | bytes 1572864 | tf_op jit(solution)/shard_map/all_to_all | solution.py:336
  12.1 6.6 %copy-start.2 = (f32[2,64,1,256]{3,2,1,0:T(1,128)S(1)}, f32[2,64,1,256]{3,2,1,0:T(1,128)}, u32[]{:S(2)}) copy-start(f32[2,64,1,256]{3,2,1,0:T(1,128)} %param.8) | copy-start | bytes 393220
  12.1 15.8 %collective-permute-start = (f32[192,256]{1,0:T(8,128)S(1)}, f32[192,256]{1,0:T(8,128)S(1)}, u32[]{:S(2)}, u32[]{:S(2)}) collective-permute-start(f32[192,256]{1,0:T(8,128)S(1)} %get-tuple-element.44), channel_id=1, source_target_pairs={{0,1},{1,0},{2,3},{3,2},{4,5},{5,4},{6,7},{7,6},{8,9},{9,8},{10,11... | collective-permute-start | bytes 589832 | tf_op jit(solution)/shard_map/ppermute | solution.py:344
  18.8 0.7 copy-start.4
  19.6 28.0 %collective-permute-start.1 = (f32[392,256]{1,0:T(8,128)S(1)}, f32[392,256]{1,0:T(8,128)S(1)}, u32[]{:S(2)}, u32[]{:S(2)}) collective-permute-start(f32[392,256]{1,0:T(8,128)S(1)} %select_maximum_fusion.own), channel_id=1, source_target_pairs={{0,1},{1,0},{2,3},{3,2},{4,5},{5,4},{6,7},{7,6},{8,9},{9,8},{10,11... | collective-permute-start | bytes 1204232 | tf_op jit(solution)/shard_map/ppermute | solution.py:344
  28.9 4.9 %copy-start.3 = (s32[64,64]{1,0:T(8,128)S(1)}, s32[64,64]{1,0:T(8,128)}, u32[]{:S(2)}) copy-start(s32[64,64]{1,0:T(8,128)} %param.13) | copy-start | bytes 49156
  28.9 19.8 %all-to-all-start.1 = ((f32[4,192,256]{2,1,0:T(8,128)}), f32[4,192,256]{2,1,0:T(8,128)S(1)}, u32[]{:S(2)}, u32[]{:S(2)}) async-start(f32[4,192,256]{2,1,0:T(8,128)} %broadcast_in_dim.32), calls=%async_computation.1 | async-start | bytes 1572864 | tf_op jit(solution)/shard_map/all_to_all | solution.py:336
  47.9 0.7 copy-start.5
  186.1 15.4 %all-to-all-start.8 = ((f32[4,64,256]{2,1,0:T(8,128)}), f32[4,64,256]{2,1,0:T(8,128)S(1)}, u32[]{:S(2)}, u32[]{:S(2)}) async-start(f32[4,64,256]{2,1,0:T(8,128)} %get-tuple-element.38), calls=%async_computation.8 | async-start | bytes 524288 | tf_op jit(solution)/shard_map/all_to_all | solution.py:336
  190.9 10.6 %collective-permute-start.2 = (f32[64,256]{1,0:T(8,128)S(1)}, f32[64,256]{1,0:T(8,128)S(1)}, u32[]{:S(2)}, u32[]{:S(2)}) collective-permute-start(f32[64,256]{1,0:T(8,128)S(1)} %get-tuple-element.36.give), channel_id=1, source_target_pairs={{0,1},{1,0},{2,3},{3,2},{4,5},{5,4},{6,7},{7,6},{8,9},{9,8},{10,11... | collective-permute-start | bytes 196616 | tf_op jit(solution)/shard_map/ppermute | solution.py:344
  198.8 11.5 %collective-permute-start.3 = (f32[64,256]{1,0:T(8,128)S(1)}, f32[64,256]{1,0:T(8,128)S(1)}, u32[]{:S(2)}, u32[]{:S(2)}) collective-permute-start(f32[64,256]{1,0:T(8,128)S(1)} %other_half.1), channel_id=1, source_target_pairs={{0,1},{1,0},{2,3},{3,2},{4,5},{5,4},{6,7},{7,6},{8,9},{9,8},{10,11... | collective-permute-start | bytes 196616 | tf_op jit(solution)/shard_map/ppermute | solution.py:344
